TPU v7x, 32 devices: a whole 2x2x4 slice. The times are simulated.
32 devices in a mesh: lat: 4 (over x, core), lon: 8 (over z, y).
Axes of the slice: x: 2, y: 2, z: 4, core: 2. Of those that a mesh axis runs over, the one named last changes fastest.
Arguments:
- field: bfloat16 [64, 256, 1024], P('lat', 'lon'), may hold values from -600 to 600
- norm_gain: float32 [1024], replicated, may hold values from 0.1 to 1.9
- w_qkv: bfloat16 [1024, 3072], replicated, may hold values from -2 to 2
- w_out: bfloat16 [1024, 1024], replicated, may hold values from -0.1875 to 0.1875
- block_cols: int32 [4, 4], replicated, may hold values from 1 to 7, as said below
- antipode: int32 [256], P('lon'), may hold values from 0 to 255, as said below
Outputs:
- update: bfloat16 [64, 256, 1024], P('lat', 'lon')
Inputs may be any that keep to these rules, and one draw needn't show every extreme that they name: `block_cols`: each row lists 4 different blocks b with |b - 4 - row| <= 3. A permutation of the longitudes; antipode[l] // 32 equals (l // 32 + 256 // 64) modulo 256 // 32.
All inputs are finite; a program needn't handle non-finite values.
Results may differ from a plain program's by a relative error of at most 0.005.
The roundings to bfloat16 on the way count: a program that leaves them out, or rounds other values in their place, can miss the bound.
Values may be sent and summed in bfloat16 or wider, within the bound.
A program may use at most 128 MiB of HBM per device.

v0:
```python
import jax
import jax.numpy as jnp
from jax import lax
from jax.sharding import PartitionSpec as P

HEADS = 16
HD = 64
HZ = 8
BM = 8


epsilon = 1e-06


def shifted(shard, axis, by):
    devices = lax.axis_size(axis)
    return lax.ppermute(shard, axis, [(i, (i + by) % devices) for i in range(devices)])


def from_partner(value, axis, distance):
    mask = 2**distance
    pairs = [(source, source ^ mask) for source in range(lax.axis_size(axis))]
    return lax.ppermute(value, axis, pairs)


def softmax_rows(scores):
    row_max = jnp.max(scores, axis=-1, keepdims=True)
    exponent = jnp.exp(scores - row_max)
    return (exponent / jnp.sum(exponent, axis=-1, keepdims=True)).astype(jnp.bfloat16)


def zonal_attend(query_rows, key_rows, value_rows):
    item_count, length, pair_width = query_rows.shape
    score_scale = HD ** (-0.5)
    query_heads = query_rows.reshape(item_count, length, 2, HD)
    key_heads = key_rows.reshape(item_count, length, 2, HD)
    value_heads = value_rows.reshape(item_count, length, 2, HD)
    block_rows = min(512, length)
    pieces = []
    for first_row in range(0, length, block_rows):
        query_block = query_heads[:, first_row : first_row + block_rows]
        scores = (
            jnp.einsum(
                "iqhd,ikhd->ihqk", query_block, key_heads, preferred_element_type=jnp.float32
            )
            * score_scale
        )
        soft_weights = softmax_rows(scores)
        result = jnp.einsum(
            "ihqk,ikhd->iqhd", soft_weights, value_heads, preferred_element_type=jnp.float32
        )
        pieces.append(result.astype(jnp.bfloat16))
    return jnp.concatenate(pieces, axis=1).reshape(item_count, length, pair_width)


def on_device(field, norm_gain, w_qkv, w_out, block_cols, antipode):
    cycle_count, lon_count, channels = field.shape
    column_heads = HEADS - HZ
    pair_count = HZ // 2
    zonal_width = HZ * HD
    score_scale = HD ** (-0.5)
    values = field.astype(jnp.float32)
    scaled = values * lax.rsqrt(jnp.mean(values * values, axis=-1, keepdims=True) + epsilon)
    normed = (scaled * norm_gain).astype(jnp.bfloat16)
    weight_split = w_qkv.reshape(channels, 3, channels)
    zonal_weight = weight_split[:, :, :zonal_width].reshape(channels, 3, pair_count, 2 * HD)
    column_weight = weight_split[:, :, zonal_width:]
    zonal_part = jnp.einsum(
        "rld,dtpc->trplc", normed, zonal_weight, preferred_element_type=jnp.float32
    )
    zonal_part = zonal_part.astype(jnp.bfloat16).reshape(
        3, cycle_count * pair_count, lon_count, 2 * HD
    )
    column_proj = jnp.einsum(
        "rld,dtc->rltc", normed, column_weight, preferred_element_type=jnp.float32
    ).astype(jnp.bfloat16)
    query_all, key_all, value_all = (
        lax.all_to_all(zonal_part[0], "lon", split_axis=0, concat_axis=1, tiled=True),
        lax.all_to_all(zonal_part[1], "lon", split_axis=0, concat_axis=1, tiled=True),
        lax.all_to_all(zonal_part[2], "lon", split_axis=0, concat_axis=1, tiled=True),
    )
    zonal_items = zonal_attend(query_all, key_all, value_all)
    returned = lax.all_to_all(zonal_items, "lon", split_axis=1, concat_axis=0, tiled=True)
    zonal_out = returned.reshape(cycle_count, pair_count, lon_count, 2 * HD)
    cap_half = lax.axis_index("lat") % 2
    lon_devices = lax.axis_size("lon")
    merged = column_proj[:, :, 1:]

    def cap_order(own_rows, other_rows):
        return jnp.where(
            cap_half == 0,
            jnp.concatenate([own_rows, other_rows], axis=0),
            jnp.concatenate([other_rows, own_rows], axis=0),
        )

    far_own = shifted(merged, "lon", lon_devices // 2)
    partner, far_partner = from_partner((merged, far_own), "lat", 0)
    cap_rows = cap_order(merged, partner)
    far_side = cap_order(far_own, far_partner)
    across = jnp.take(far_side, antipode % lon_count, axis=1)[::-1]
    column = jnp.concatenate([across, cap_rows], axis=0)
    block_total = column.shape[0] // BM
    column = column.reshape(block_total, BM, lon_count, 2, column_heads, HD)
    picks_per_row = block_cols.shape[1]
    local_blocks = cycle_count // BM
    pieces = []
    for local_block in range(local_blocks):
        block_row = cap_half * local_blocks + local_block
        picked = lax.dynamic_index_in_dim(block_cols, block_row, 0, keepdims=False)
        chosen = jnp.take(column, picked, axis=0).reshape(
            picks_per_row * BM, lon_count, 2, column_heads, HD
        )
        query_block = column_proj[local_block * BM : (local_block + 1) * BM, :, 0]
        query_block = query_block.reshape(BM, lon_count, column_heads, HD)
        scores = (
            jnp.einsum(
                "qlhd,klhd->lhqk", query_block, chosen[:, :, 0], preferred_element_type=jnp.float32
            )
            * score_scale
        )
        soft_weights = softmax_rows(scores)
        result = jnp.einsum(
            "lhqk,klhd->qlhd", soft_weights, chosen[:, :, 1], preferred_element_type=jnp.float32
        )
        pieces.append(result.astype(jnp.bfloat16).reshape(BM, lon_count, column_heads * HD))
    meridional = jnp.concatenate(pieces, axis=0)
    zonal_rows_out = w_out[:zonal_width].reshape(pair_count, 2 * HD, channels)
    total = jnp.einsum(
        "rplc,pce->rle", zonal_out, zonal_rows_out, preferred_element_type=jnp.float32
    )
    total = total + jnp.einsum(
        "rlc,ce->rle", meridional, w_out[zonal_width:], preferred_element_type=jnp.float32
    )
    return total.astype(jnp.bfloat16)


def solution(mesh):
    in_specs = (P("lat", "lon", None), P(), P(), P(), P(), P("lon"))
    out_specs = P("lat", "lon", None)
    return jax.shard_map(
        on_device, mesh=mesh, in_specs=in_specs, out_specs=out_specs, check_vma=False
    )
```

profile of v0, /device:TPU:0, one launch (start us, length us, event | category | flops | bytes accessed | tf_op | source)
XLA Modules:
  0.0 214.1 jit_solution(12262498181520285386)
XLA Ops:
  0.0 1.5 fusion.7
  1.5 8.6 %copy.53 = bf16[1024,3072]{0,1:T(8,128)(2,1)} copy(bf16[1024,3072]{1,0:T(8,128)(2,1)} %param.10) | data formatting | bytes 12582912 | tf_op args[2]
  10.1 2.3 %slice.65 = bf16[1024,3,512]{0,2,1:T(8,128)(2,1)S(1)} slice(bf16[1024,3,1024]{0,2,1:T(8,128)(2,1)} %bitcast.123), slice={[0:1024], [0:3], [0:512]} | slice | bytes 6291456 | tf_op jit(solution)/shard_map/slice | solution.py:66
  12.4 0.0 copy-done.5
  12.4 0.0 copy-done.7
  12.4 1.9 fusion.19
  14.4 1.1 fusion.52
  15.5 21.6 %all_to_all.60 = bf16[64,32,128]{2,1,0:T(8,128)(2,1)S(1)} all-to-all(bf16[64,32,128]{2,1,0:T(8,128)(2,1)S(1)} %bitcast.137), channel_id=1, replica_groups=mesh['lat'=4,'lon'=8] {'lon'}, dimensions={0} | all-to-all | bytes 1048576 | tf_op jit(solution)/shard_map/all_to_all | solution.py:79
  37.1 17.5 %all_to_all.61 = bf16[64,32,128]{2,1,0:T(8,128)(2,1)S(1)} all-to-all(bf16[64,32,128]{2,1,0:T(8,128)(2,1)S(1)} %bitcast.136), channel_id=1, replica_groups=mesh['lat'=4,'lon'=8] {'lon'}, dimensions={0} | all-to-all | bytes 1048576 | tf_op jit(solution)/shard_map/all_to_all | solution.py:80
  54.6 3.6 %all-to-all-start.1 = ((bf16[64,32,128]{2,1,0:T(8,128)(2,1)}), bf16[64,32,128]{2,1,0:T(8,128)(2,1)S(1)}, u32[]{:S(2)}, u32[]{:S(2)}) async-start(bf16[64,32,128]{2,1,0:T(8,128)(2,1)} %bitcast.9), calls=%async_computation.1 | async-start | bytes 1048576 | tf_op jit(solution)/shard_map/all_to_all | solution.py:78
  58.3 3.8 %fusion.18 = bf16[16,32,3,512]{3,1,2,0:T(8,128)(2,1)S(1)} fusion(bf16[1024,3,1024]{0,2,1:T(8,128)(2,1)} %bitcast.124, bf16[16,32,1024]{2,1,0:T(8,128)(2,1)S(1)} %copy-done.5, f32[1024]{0:T(1024)S(1)} %copy-done.7, f32[16,32]{1,0:T(8,128)S(1)} %add_rsqrt_fusion), kind=kOutput, calls=%fused_computation.38 | convolution fusion | flops 1613496320 | bytes 5773312 | tf_op jit(solution)/shard_map/rld,dtc->rltc/dot_general | solution.py:74
  62.1 0.0 copy-start.3
  62.1 0.1 slice.70
  62.2 0.1 collective-permute-start.2
  62.3 3.0 %collective-permute-start = (bf16[16,32,2,512]{3,1,2,0:T(8,128)(2,1)S(1)}, bf16[16,32,2,512]{3,1,2,0:T(8,128)(2,1)}, u32[]{:S(2)}, u32[]{:S(2)}) collective-permute-start(bf16[16,32,2,512]{3,1,2,0:T(8,128)(2,1)S(1)} %slice.70), channel_id=1, source_target_pairs={{0,4},{1,5},{2,6},{3,7},{4,0},{5,1},{6,2},{7,3},{8,12},{9,13},{10,... | collective-permute-start | bytes 3145736 | tf_op jit(solution)/shard_map/ppermute | solution.py:17
  65.3 0.8 copy.57
  66.1 0.0 copy-done.3
  66.1 30.4 %all-to-all-done.1 = bf16[64,32,128]{2,1,0:T(8,128)(2,1)S(1)} async-done(((bf16[64,32,128]{2,1,0:T(8,128)(2,1)}), bf16[64,32,128]{2,1,0:T(8,128)(2,1)S(1)}, u32[]{:S(2)}, u32[]{:S(2)}) %all-to-all-start.1) | async-done | bytes 524320 | tf_op jit(solution)/shard_map/all_to_all | solution.py:78
  96.6 0.4 reshape.78
  97.0 1.4 reshape.77
  98.4 2.4 %reshape.79 = bf16[8,256,2,64]{3,2,1,0:T(2,128)(2,1)S(1)} reshape(bf16[8,8,32,128]{3,2,1,0:T(8,128)(2,1)} %copy.57) | data formatting | bytes 1048576 | tf_op jit(solution)/shard_map/reshape | solution.py:36
  100.9 0.7 fusion.36
  101.6 0.0 copy-start.4
  101.6 3.2 %fusion.56 = (f32[8,2,256]{2,1,0:T(2,128)S(1)}, f32[8,2,256,256]{2,3,1,0:T(8,128)S(1)}) fusion(f32[8,2,256,256]{2,3,1,0:T(8,128)S(1)} %fusion.36), kind=kOutput, calls=%fused_computation.90 | output fusion | flops 4194559 | bytes 8404992 | tf_op jit(solution)/shard_map/sub | solution.py:28
  104.8 0.5 fusion.28
  105.4 1.1 copy.62
  106.5 3.7 %all-to-all-start.3 = ((bf16[8,256,128]{2,0,1:T(8,128)(2,1)}), bf16[8,256,128]{2,0,1:T(8,128)(2,1)S(1)}, u32[]{:S(2)}, u32[]{:S(2)}) async-start(bf16[8,256,128]{2,0,1:T(8,128)(2,1)} %copy.62), calls=%async_computation.3 | async-start | bytes 1048576 | tf_op jit(solution)/shard_map/all_to_all | solution.py:83
  110.1 14.7 %collective-permute-done = bf16[16,32,2,512]{3,1,2,0:T(8,128)(2,1)} collective-permute-done((bf16[16,32,2,512]{3,1,2,0:T(8,128)(2,1)S(1)}, bf16[16,32,2,512]{3,1,2,0:T(8,128)(2,1)}, u32[]{:S(2)}, u32[]{:S(2)}) %collective-permute-start) | collective-permute-done | bytes 1048608 | tf_op jit(solution)/shard_map/ppermute | solution.py:17
  124.8 0.0 collective-permute-start.1
  124.8 1.1 fusion.53
  125.9 0.0 copy-start.6
  125.9 0.0 copy-start.8
  125.9 0.3 reshape_squeeze.6
  126.2 0.3 reshape_squeeze.7
  126.5 0.1 copy-done.6
  126.6 0.0 copy-done.8
  126.6 0.0 collective-permute-done.2
  126.6 3.2 %maximum_select_fusion.1 = bf16[32,32,2,512]{3,1,2,0:T(8,128)(2,1)} fusion(bf16[16,32,2,512]{3,1,2,0:T(8,128)(2,1)} %collective-permute-done.2, bf16[16,32,2,512]{3,1,2,0:T(8,128)(2,1)S(1)} %slice.70, pred[]{:T(512)S(6)} %eq.8), kind=kLoop, calls=%fused_computation.31 | loop fusion | flops 3145728 | bytes 4194305 | tf_op jit(solution)/shard_map/jit(_where)/select_n | solution.py:90
  129.9 0.0 all-to-all-done.3
  129.9 0.9 copy.64
  130.8 0.0 collective-permute-done.1
  130.8 2.6 %maximum_select_fusion = bf16[32,32,2,512]{3,1,2,0:T(8,128)(2,1)S(1)} fusion(bf16[16,32,2,512]{3,1,2,0:T(8,128)(2,1)} %collective-permute-done.1, bf16[16,32,2,512]{3,1,2,0:T(8,128)(2,1)} %collective-permute-done, pred[]{:T(512)S(6)} %eq.8), kind=kLoop, calls=%fused_computation.30 | loop fusion | flops 3145728 | bytes 4194305 | tf_op jit(solution)/shard_map/jit(_where)/select_n | solution.py:90
  133.4 2.5 %copy.66 = bf16[32,32,2,512]{3,0,2,1:T(8,128)(2,1)} copy(bf16[32,32,2,512]{3,1,2,0:T(8,128)(2,1)S(1)} %maximum_select_fusion) | data formatting | bytes 4194304 | tf_op jit(solution)/shard_map/jit(_where)/select_n | solution.py:90
  135.8 2.3 %gather_fusion = bf16[32,32,2,512]{3,1,2,0:T(8,128)(2,1)S(1)} fusion(bf16[32,32,2,512]{3,0,2,1:T(8,128)(2,1)} %copy.66, s32[1024]{0:T(1024)S(1)} %pad_clamp_fusion.2), kind=kCustom, calls=%fused_computation.2 | custom fusion | bytes 4194432 | tf_op jit(solution)/shard_map/jit(_take)/gather | solution.py:100
  138.1 3.8 %fusion.15 = bf16[32,32,2,512]{3,1,2,0:T(8,128)(2,1)} fusion(bf16[32,32,2,512]{3,1,2,0:T(8,128)(2,1)S(1)} %gather_fusion, pred[32]{0:T(512)(128)(4,1)S(1)} %get-tuple-element.10), kind=kLoop, calls=%fused_computation.35 | loop fusion | flops 1048576 | bytes 4194336 | tf_op jit(solution)/shard_map/jit(_take)/select_n | solution.py:100
  141.9 3.3 %rev.3 = bf16[32,32,2,512]{3,1,2,0:T(8,128)(2,1)} reverse(bf16[32,32,2,512]{3,1,2,0:T(8,128)(2,1)} %fusion.15), dimensions={0} | reverse | bytes 4194304 | tf_op jit(solution)/shard_map/rev | solution.py:100
  145.1 0.0 copy-done
  145.1 3.9 %pad_maximum_fusion = bf16[64,32,2,512]{3,1,2,0:T(8,128)(2,1)} fusion(bf16[32,32,2,512]{3,1,2,0:T(8,128)(2,1)S(1)} %copy-done, bf16[32,32,2,512]{3,1,2,0:T(8,128)(2,1)} %rev.3), kind=kLoop, calls=%fused_computation.6 | loop fusion | flops 2097152 | bytes 8388608 | tf_op jit(solution)/shard_map/concatenate | solution.py:101
  149.1 11.2 %reshape.83 = bf16[8,8,32,2,8,64]{5,4,2,3,1,0:T(8,128)(2,1)} reshape(bf16[64,32,2,512]{3,1,2,0:T(8,128)(2,1)} %pad_maximum_fusion) | data formatting | bytes 8388608 | tf_op jit(solution)/shard_map/reshape | solution.py:103
  160.3 6.4 %gather_fusion.2 = bf16[4,8,32,2,8,64]{5,4,2,3,1,0:T(8,128)(2,1)} fusion(bf16[8,8,32,2,8,64]{5,4,2,3,1,0:T(8,128)(2,1)} %reshape.83, s32[1024]{0:T(1024)S(1)} %pad_clamp_fusion), kind=kCustom, calls=%fused_computation.1.clone | custom fusion | bytes 4194320 | tf_op jit(solution)/shard_map/jit(_take)/gather | solution.py:110
  166.7 6.4 %gather_fusion.1 = bf16[4,8,32,2,8,64]{5,4,2,3,1,0:T(8,128)(2,1)} fusion(bf16[8,8,32,2,8,64]{5,4,2,3,1,0:T(8,128)(2,1)} %reshape.83, s32[1024]{0:T(1024)S(1)} %pad_clamp_fusion.1), kind=kCustom, calls=%fused_computation.clone | custom fusion | bytes 4194320 | tf_op jit(solution)/shard_map/jit(_take)/gather | solution.py:110
  173.1 6.2 %broadcast_select_fusion = (bf16[4,8,32,2,8,64]{5,4,2,3,1,0:T(8,128)(2,1)S(1)}, bf16[4,8,32,2,8,64]{5,4,2,3,1,0:T(8,128)(2,1)}) fusion(bf16[4,8,32,2,8,64]{5,4,2,3,1,0:T(8,128)(2,1)} %gather_fusion.2, pred[4]{0:T(512)(128)(4,1)S(1)} %get-tuple-element.17, bf16[4,8,32,2,8,64]{5,4,2,3,1,0:T(8,128)(2,1)} %gather_fusion.1, pred[4]{0:T(512)(128)(4,1)S(1)} %get-tuple-element.6), kind=kLoop, calls=%fused_computation.11 | loop fusion | flops 2097152 | bytes 8388616 | tf_op jit(solution)/shard_map/jit(_take)/select_n | solution.py:110
  179.3 6.8 %copy.101 = bf16[4,8,32,2,8,64]{5,1,0,4,2,3:T(8,128)(2,1)} copy(bf16[4,8,32,2,8,64]{5,4,2,3,1,0:T(8,128)(2,1)S(1)} %get-tuple-element.25) | data formatting | bytes 4194304 | tf_op jit(solution)/shard_map/jit(_take)/select_n | solution.py:110
  186.1 3.0 %fusion.54 = (f32[32,8,8]{2,1,0:T(8,128)S(1)}, f32[32,8,8,32]{3,2,1,0:T(8,128)S(1)}) fusion(bf16[32,32,2,8,64]{4,0,3,1,2:T(8,128)(2,1)} %bitcast.125, bf16[8,32,8,64]{3,2,1,0:T(8,128)(2,1)S(1)} %reshape_squeeze.7), kind=kOutput, calls=%fused_computation.88 | convolution fusion | flops 8585247 | bytes 2629632 | tf_op jit(solution)/shard_map/sub | solution.py:28
  189.1 2.3 %fusion.29 = bf16[8,32,8,64]{3,0,2,1:T(8,128)(2,1)S(1)} fusion(bf16[32,32,2,8,64]{4,0,3,1,2:T(8,128)(2,1)} %bitcast.126, f32[32,8,8,32]{3,2,1,0:T(8,128)S(1)} %get-tuple-element.20, f32[32,8,8]{2,1,0:T(8,128)S(1)} %get-tuple-element.19), kind=kOutput, calls=%fused_computation.50 | convolution fusion | flops 8650752 | bytes 2629632 | tf_op jit(solution)/shard_map/lhqk,klhd->qlhd/dot_general | solution.py:122
  191.4 0.1 copy.73
  191.5 0.3 reshape.87
  191.8 9.2 %copy.102 = bf16[4,8,32,2,8,64]{5,1,0,4,2,3:T(8,128)(2,1)} copy(bf16[4,8,32,2,8,64]{5,4,2,3,1,0:T(8,128)(2,1)} %get-tuple-element.26) | data formatting | bytes 4194304 | tf_op jit(solution)/shard_map/jit(_take)/select_n | solution.py:110
  201.0 3.9 %fusion.55 = (f32[32,8,8]{2,1,0:T(8,128)S(1)}, f32[32,8,8,32]{3,2,1,0:T(8,128)}) fusion(bf16[32,32,2,8,64]{4,0,3,1,2:T(8,128)(2,1)} %bitcast.127, bf16[8,32,8,64]{3,2,1,0:T(8,128)(2,1)S(1)} %reshape_squeeze.6), kind=kOutput, calls=%fused_computation.89 | convolution fusion | flops 8585247 | bytes 2629632 | tf_op jit(solution)/shard_map/sub | solution.py:28
  204.9 2.7 %fusion.30 = bf16[8,32,8,64]{3,0,2,1:T(8,128)(2,1)S(1)} fusion(bf16[32,32,2,8,64]{4,0,3,1,2:T(8,128)(2,1)} %bitcast.128, f32[32,8,8,32]{3,2,1,0:T(8,128)} %get-tuple-element.22, f32[32,8,8]{2,1,0:T(8,128)S(1)} %get-tuple-element.21), kind=kOutput, calls=%fused_computation.51 | convolution fusion | flops 8650752 | bytes 3416064 | tf_op jit(solution)/shard_map/lhqk,klhd->qlhd/dot_general | solution.py:122
  207.6 0.9 copy.70
  208.5 2.2 %reshape.85 = bf16[8,32,512]{2,1,0:T(8,128)(2,1)} reshape(bf16[8,32,8,64]{3,2,1,0:T(8,128)(2,1)} %copy.70) | data formatting | bytes 524288 | tf_op jit(solution)/shard_map/reshape | solution.py:125
  210.7 1.7 fusion.33
  212.4 1.7 fusion.14
  (18 shorter events, 0.1 us)
Async XLA Ops:
  10.1 2.3 %copy-start.5 = (bf16[16,32,1024]{2,1,0:T(8,128)(2,1)S(1)}, bf16[16,32,1024]{2,1,0:T(8,128)(2,1)}, u32[]{:S(2)}) copy-start(bf16[16,32,1024]{2,1,0:T(8,128)(2,1)} %param.8) | copy-start | bytes 3145732
  10.1 2.3 %copy-start.7 = (f32[1024]{0:T(1024)S(1)}, f32[1024]{0:T(1024)}, u32[]{:S(2)}) copy-start(f32[1024]{0:T(1024)} %param.9) | copy-start | bytes 12292
  54.6 41.9 %all-to-all-start.1 = ((bf16[64,32,128]{2,1,0:T(8,128)(2,1)}), bf16[64,32,128]{2,1,0:T(8,128)(2,1)S(1)}, u32[]{:S(2)}, u32[]{:S(2)}) async-start(bf16[64,32,128]{2,1,0:T(8,128)(2,1)} %bitcast.9), calls=%async_computation.1 | async-start | bytes 1048576 | tf_op jit(solution)/shard_map/all_to_all | solution.py:78
  62.1 4.0 %copy-start.3 = (bf16[16,32,3,512]{3,1,2,0:T(8,128)(2,1)}, bf16[16,32,3,512]{3,1,2,0:T(8,128)(2,1)S(1)}, u32[]{:S(2)}) copy-start(bf16[16,32,3,512]{3,1,2,0:T(8,128)(2,1)S(1)} %fusion.18) | copy-start | bytes 4718596
  62.2 64.4 %collective-permute-start.2 = (bf16[16,32,2,512]{3,1,2,0:T(8,128)(2,1)S(1)}, bf16[16,32,2,512]{3,1,2,0:T(8,128)(2,1)}, u32[]{:S(2)}, u32[]{:S(2)}) collective-permute-start(bf16[16,32,2,512]{3,1,2,0:T(8,128)(2,1)S(1)} %slice.70), channel_id=1, source_target_pairs={{0,8},{8,0},{16,24},{24,16},{1,9},{9,1},{17,25},{25,17},{2,10},{10... | collective-permute-start | bytes 3145736 | tf_op jit(solution)/shard_map/ppermute | solution.py:23
  62.3 62.5 %collective-permute-start = (bf16[16,32,2,512]{3,1,2,0:T(8,128)(2,1)S(1)}, bf16[16,32,2,512]{3,1,2,0:T(8,128)(2,1)}, u32[]{:S(2)}, u32[]{:S(2)}) collective-permute-start(bf16[16,32,2,512]{3,1,2,0:T(8,128)(2,1)S(1)} %slice.70), channel_id=1, source_target_pairs={{0,4},{1,5},{2,6},{3,7},{4,0},{5,1},{6,2},{7,3},{8,12},{9,13},{10,... | collective-permute-start | bytes 3145736 | tf_op jit(solution)/shard_map/ppermute | solution.py:17
  101.6 3.3 %copy-start.4 = (bf16[8,256,2,64]{3,2,1,0:T(2,128)(2,1)S(1)}, bf16[8,256,2,64]{3,2,1,0:T(2,128)(2,1)}, u32[]{:S(2)}) copy-start(bf16[8,256,2,64]{3,2,1,0:T(2,128)(2,1)} %reshape.77) | copy-start | bytes 1572868
  106.5 23.4 %all-to-all-start.3 = ((bf16[8,256,128]{2,0,1:T(8,128)(2,1)}), bf16[8,256,128]{2,0,1:T(8,128)(2,1)S(1)}, u32[]{:S(2)}, u32[]{:S(2)}) async-start(bf16[8,256,128]{2,0,1:T(8,128)(2,1)} %copy.62), calls=%async_computation.3 | async-start | bytes 1048576 | tf_op jit(solution)/shard_map/all_to_all | solution.py:83
  124.8 6.0 %collective-permute-start.1 = (bf16[16,32,2,512]{3,1,2,0:T(8,128)(2,1)}, bf16[16,32,2,512]{3,1,2,0:T(8,128)(2,1)}, u32[]{:S(2)}, u32[]{:S(2)}) collective-permute-start(bf16[16,32,2,512]{3,1,2,0:T(8,128)(2,1)} %collective-permute-done), channel_id=1, source_target_pairs={{0,8},{8,0},{16,24},{24,16},{1,9},{9,1},{17,25},{25,17},{2,10},{10... | collective-permute-start | bytes 3145736 | tf_op jit(solution)/shard_map/ppermute | solution.py:23
  125.9 0.7 copy-start.6
  125.9 0.7 copy-start.8
  141.8 3.3 %copy-start = (bf16[32,32,2,512]{3,1,2,0:T(8,128)(2,1)S(1)}, bf16[32,32,2,512]{3,1,2,0:T(8,128)(2,1)}, u32[]{:S(2)}) copy-start(bf16[32,32,2,512]{3,1,2,0:T(8,128)(2,1)} %maximum_select_fusion.1) | copy-start | bytes 6291460
  204.9 5.8 %copy-start.1 = (bf16[1024,1024]{1,0:T(8,128)(2,1)S(1)}, bf16[1024,1024]{1,0:T(8,128)(2,1)}, u32[]{:S(2)}) copy-start(bf16[1024,1024]{1,0:T(8,128)(2,1)} %param.11) | copy-start | bytes 6291460
  208.5 3.9 %slice-start = ((bf16[1024,1024]{1,0:T(8,128)(2,1)}), bf16[512,1024]{1,0:T(8,128)(2,1)S(1)}, s32[]{:S(2)}) async-start(bf16[1024,1024]{1,0:T(8,128)(2,1)} %param.11), calls=%async_computation.4 | async-start | bytes 2097152 | tf_op jit(solution)/shard_map/slice | solution.py:127
  210.7 1.7 copy-start.2
where the time goes:
time: 215 us; the launch traced here: 214 us
  local copies, waits for them, and re-layouts  72.5 us (34%)
  waiting for transfers between devices  45.1 us (21%)
  blocking collectives  39.2 us (18%)
  other arithmetic  24.5 us (11%)
  matrix products  22.2 us (10%)
  starting transfers between devices  10.4 us (5%)
    all_to_all x1, waiting for transfers between devices, on_device(): lax.all_to_all(zonal_part[0], 'lon', split_axis=0, concat_axis=1, tiled=T...  30.4 us
    all_to_all x1, blocking collectives, on_device(): lax.all_to_all(zonal_part[1], 'lon', split_axis=0, concat_axis=1, tiled=T...  21.6 us
    all_to_all x1, blocking collectives, on_device(): lax.all_to_all(zonal_part[2], 'lon', split_axis=0, concat_axis=1, tiled=T...  17.5 us
    select_n x2, local copies, waits for them, and re-layouts, on_device(): jnp.take(column, picked, axis=0)  16 us
    ppermute x1, waiting for transfers between devices, shifted(): lax.ppermute(shard, axis, [(i, (i + by) % devices) for i in range(devices)])  14.7 us
    gather x2, local copies, waits for them, and re-layouts, on_device(): jnp.take(column, picked, axis=0)  12.8 us
    reshape x1, local copies, waits for them, and re-layouts, on_device(): column = column.reshape(block_total, BM, lon_count, 2, column_heads, HD)  11.2 us
    unnamed x19, local copies, waits for them, and re-layouts  8.72 us
  transfers between devices with their start and end apart: 5, of which 2 were waited for; matrix products, arithmetic and copies ran while one was open for 10% of the time, Pallas kernels for 0%

commit v1 on v0

--- a/solution.py
+++ b/solution.py
@@ -1,6 +1,10 @@
+import functools
+
 import jax
 import jax.numpy as jnp
 from jax import lax
+from jax.experimental import pallas as pl
+from jax.experimental.pallas import tpu as pltpu
 from jax.sharding import PartitionSpec as P
 
 HEADS = 16
@@ -134,9 +138,329 @@
     return total.astype(jnp.bfloat16)
 
 
+GROUP = 4
+MESH = pl.DeviceIdType.MESH
+
+
+def places():
+    lat, lon = lax.axis_index("lat"), lax.axis_index("lon")
+    half, q = lon // GROUP, lon % GROUP
+    return lat, lon, half, q
+
+
+def exchange_kernel(x_ref, xz_ref, part_ref, far_ref, farpart_ref, send, recv, local):
+    lat, lon, half, q = places()
+    anti = (1 - half) * GROUP + q
+    mate = lat + 1 - 2 * (lat % 2)
+    rows = x_ref.shape[0] // GROUP
+
+    def peer(k):
+        return (q + k) % GROUP
+
+    def chunk(ref, p):
+        return ref.at[pl.ds(p * rows, rows)]
+
+    def remote(src, dst, n, lat_id, lon_id):
+        return pltpu.make_async_remote_copy(
+            src_ref=src,
+            dst_ref=dst,
+            send_sem=send.at[n],
+            recv_sem=recv.at[n],
+            device_id=(lat_id, lon_id),
+            device_id_type=MESH,
+        )
+
+    barrier = pltpu.get_barrier_semaphore()
+    partners = [(lat, anti), (mate, lon)] + [(lat, half * GROUP + peer(k)) for k in (1, 2, 3)]
+    for a, b in partners:
+        pl.semaphore_signal(barrier, inc=1, device_id=(a, b), device_id_type=MESH)
+    pl.semaphore_wait(barrier, len(partners))
+
+    order = (1, 2, 3, 0)
+    far = [remote(chunk(x_ref, peer(k)), chunk(far_ref, peer(k)), n, lat, anti) for n, k in enumerate(order)]
+    near = [
+        remote(chunk(x_ref, peer(k)), xz_ref.at[0, q], 3 + k, lat, half * GROUP + peer(k))
+        for k in (1, 2, 3)
+    ]
+    pair = remote(x_ref, part_ref, 7, mate, lon)
+    for copy in far + near + [pair]:
+        copy.start()
+    own = pltpu.make_async_copy(chunk(x_ref, q), xz_ref.at[0, q], local.at[0])
+    own.start()
+    later = []
+    for n, k in enumerate(order):
+        far[n].wait_recv()
+        got = chunk(far_ref, peer(k))
+        if k:
+            on = remote(got, xz_ref.at[1, q], 7 + k, lat, half * GROUP + peer(k))
+        else:
+            on = pltpu.make_async_copy(got, xz_ref.at[1, q], local.at[1])
+        on.start()
+        across = remote(got, chunk(farpart_ref, peer(k)), 11 + n, mate, lon)
+        across.start()
+        later += [on, across]
+    for copy in far:
+        copy.wait_send()
+    for copy in near + [pair, own] + later:
+        copy.wait()
+
+
+def exchange(field):
+    cycles, lons, width = field.shape
+    like = jax.ShapeDtypeStruct(field.shape, field.dtype)
+    return pl.pallas_call(
+        exchange_kernel,
+        name="exchange",
+        out_shape=(
+            jax.ShapeDtypeStruct((2, GROUP, cycles // GROUP, lons, width), field.dtype),
+            like,
+            like,
+            like,
+        ),
+        in_specs=[pl.BlockSpec(memory_space=pl.ANY)],
+        out_specs=[pl.BlockSpec(memory_space=pl.ANY)] * 4,
+        scratch_shapes=[
+            pltpu.SemaphoreType.DMA((15,)),
+            pltpu.SemaphoreType.DMA((15,)),
+            pltpu.SemaphoreType.DMA((2,)),
+        ],
+        compiler_params=pltpu.CompilerParams(collective_id=0, has_side_effects=True),
+    )(field)
+
+
+def giveback_kernel(z_ref, out_ref, send, recv, local):
+    lat, lon, half, q = places()
+    rows = out_ref.shape[0] // GROUP
+    barrier = pltpu.get_barrier_semaphore()
+    peers = [(q + k) % GROUP for k in (1, 2, 3)]
+    for p in peers:
+        pl.semaphore_signal(barrier, inc=1, device_id=(lat, half * GROUP + p), device_id_type=MESH)
+    pl.semaphore_wait(barrier, 3)
+    mine = out_ref.at[pl.ds(q * rows, rows)]
+    copies = [
+        pltpu.make_async_remote_copy(
+            src_ref=z_ref.at[p],
+            dst_ref=mine,
+            send_sem=send.at[n],
+            recv_sem=recv.at[n],
+            device_id=(lat, half * GROUP + p),
+            device_id_type=MESH,
+        )
+        for n, p in enumerate(peers)
+    ]
+    copies.append(pltpu.make_async_copy(z_ref.at[q], mine, local))
+    for copy in copies:
+        copy.start()
+    for copy in copies:
+        copy.wait()
+
+
+def giveback(zonal):
+    group, rows, lons, width = zonal.shape
+    return pl.pallas_call(
+        giveback_kernel,
+        name="giveback",
+        out_shape=jax.ShapeDtypeStruct((group * rows, lons, width), zonal.dtype),
+        in_specs=[pl.BlockSpec(memory_space=pl.ANY)],
+        out_specs=pl.BlockSpec(memory_space=pl.ANY),
+        scratch_shapes=[
+            pltpu.SemaphoreType.DMA((3,)),
+            pltpu.SemaphoreType.DMA((3,)),
+            pltpu.SemaphoreType.DMA,
+        ],
+        compiler_params=pltpu.CompilerParams(collective_id=1, has_side_effects=True),
+    )(zonal)
+
+
+def norm_rows(x, gain):
+    values = x.astype(jnp.float32)
+    mean = jnp.mean(values * values, axis=-1, keepdims=True)
+    return (values * lax.rsqrt(mean + epsilon) * gain).astype(jnp.bfloat16)
+
+
+def mm(a, b):
+    return jnp.dot(a, b, preferred_element_type=jnp.float32).astype(jnp.bfloat16)
+
+
+def pair_attend(q, k, v, mask):
+    rows = q.shape[0]
+    first = lax.broadcasted_iota(jnp.int32, q.shape, 1) < HD
+    q = q * jnp.asarray(HD ** (-0.5), q.dtype)
+    zero = jnp.zeros_like(q)
+    stacked = jnp.concatenate([jnp.where(first, q, zero), jnp.where(first, zero, q)], axis=0)
+    scores = lax.dot_general(stacked, k, (((1,), (1,)), ((), ())), preferred_element_type=jnp.float32)
+    if mask is not None:
+        scores = jnp.where(mask, scores, -jnp.inf)
+    exponent = jnp.exp(scores - jnp.max(scores, axis=-1, keepdims=True))
+    weights = (exponent * (1.0 / jnp.sum(exponent, axis=-1, keepdims=True))).astype(jnp.bfloat16)
+    out = jnp.dot(weights, v, preferred_element_type=jnp.float32)
+    return jnp.where(first, out[:rows], out[rows:]).astype(jnp.bfloat16)
+
+
+STEP = 256
+
+
+def attend_kernel(
+    slots_ref, x_ref, part_ref, far_ref, farpart_ref, xz_ref, gain_ref, w_ref, own_ref, ant_ref,
+    zo_ref, col_ref, xn, kc, vc, qc, kz, vz, qz, oc,
+):
+    gain = gain_ref[...]
+    tokens = x_ref.shape[0]
+    width = x_ref.shape[1]
+    part = HZ * HD
+
+    def weight(which, side):
+        first = which * width + side * part
+        return w_ref[:, first : first + part]
+
+    for s, (ref, order) in enumerate(
+        ((x_ref, own_ref), (part_ref, own_ref), (far_ref, ant_ref), (farpart_ref, ant_ref))
+    ):
+        @pl.loop(0, tokens // 64)
+        def _(i):
+            at = pl.ds(pl.multiple_of(i * 64, 64), 64)
+            xn[at, :] = norm_rows(ref[at, :], gain)
+
+        @pl.loop(0, tokens // STEP)
+        def _(i):
+            at = pl.ds(pl.multiple_of(i * STEP, STEP), STEP)
+            hit = lax.broadcasted_iota(jnp.int32, (STEP, tokens), 1) == order[at, :]
+            placed = mm(jnp.where(hit, 1.0, 0.0).astype(jnp.bfloat16), xn[...])
+            to = pl.ds(pl.multiple_of(s * tokens + i * STEP, STEP), STEP)
+            kc[to, :] = mm(placed, weight(1, 1))
+            vc[to, :] = mm(placed, weight(2, 1))
+            if s == 0:
+                qc[at, :] = mm(placed, weight(0, 1))
+
+    @pl.loop(0, xz_ref.shape[0] // STEP)
+    def _(i):
+        for j in range(STEP // 64):
+            at = pl.ds(pl.multiple_of(i * STEP + j * 64, 64), 64)
+            xn[j * 64 : (j + 1) * 64, :] = norm_rows(xz_ref[at, :], gain)
+        at = pl.ds(pl.multiple_of(i * STEP, STEP), STEP)
+        placed = xn[0:STEP, :]
+        kz[at, :] = mm(placed, weight(1, 0))
+        vz[at, :] = mm(placed, weight(2, 0))
+
+        @pl.when(i * STEP < tokens)
+        def _():
+            qz[at, :] = mm(placed, weight(0, 0))
+
+    rows = BM * 8
+    groups = tokens // (2 * rows)
+    mask = (
+        lax.broadcasted_iota(jnp.int32, (2 * rows, 4 * rows), 0) % 8
+        == lax.broadcasted_iota(jnp.int32, (2 * rows, 4 * rows), 1) % 8
+    )
+
+    @pl.loop(0, 2 * groups)
+    def _(n):
+        block, g = n // groups, n % groups
+        at = pl.ds(pl.multiple_of(n * rows, rows), rows)
+        picks = [
+            pl.ds(pl.multiple_of((slots_ref[block, m] * groups + g) * rows, rows), rows) for m in range(4)
+        ]
+        for p in range(part // 128):
+            cols = slice(p * 128, (p + 1) * 128)
+            k = jnp.concatenate([kc[pick, cols] for pick in picks], axis=0)
+            v = jnp.concatenate([vc[pick, cols] for pick in picks], axis=0)
+            oc[at, cols] = pair_attend(qc[at, cols], k, v, mask)
+
+    @pl.loop(0, tokens // STEP)
+    def _(i):
+        at = pl.ds(pl.multiple_of(i * STEP, STEP), STEP)
+        token = lax.broadcasted_iota(jnp.int32, (STEP, tokens), 0) + i * STEP
+        place = lax.broadcasted_iota(jnp.int32, (STEP, tokens), 1)
+        lons = 8 * groups
+        cycle, l = token // lons, token % lons
+        want = (((cycle // BM) * groups + l // 8) * BM + cycle % BM) * 8 + l % 8
+        col_ref[at, :] = mm(jnp.where(want == place, 1.0, 0.0).astype(jnp.bfloat16), oc[...])
+
+    lons = 8 * groups
+    per = xz_ref.shape[0] // (2 * GROUP * lons)
+
+    @pl.loop(0, per)
+    def _(c):
+        def gather(ref, cols, many):
+            return jnp.concatenate(
+                [ref[pl.ds(pl.multiple_of((m * per + c) * lons, lons), lons), cols] for m in range(many)],
+                axis=0,
+            )
+
+        for p in range(part // 128):
+            cols = slice(p * 128, (p + 1) * 128)
+            out = pair_attend(
+                gather(qz, cols, GROUP), gather(kz, cols, 2 * GROUP), gather(vz, cols, 2 * GROUP), None
+            )
+            for m in range(GROUP):
+                to = pl.ds(pl.multiple_of((m * per + c) * lons, lons), lons)
+                zo_ref[to, cols] = out[m * lons : (m + 1) * lons]
+
+
+def attend(slots, x, part, far, farpart, xz, gain, w_qkv, own, ant):
+    tokens, width = x.shape
+    side = HZ * HD
+    bf = jnp.bfloat16
+    vmem = pl.BlockSpec(memory_space=pltpu.VMEM)
+    return pl.pallas_call(
+        attend_kernel,
+        name="attend",
+        out_shape=(jax.ShapeDtypeStruct((tokens, side), bf), jax.ShapeDtypeStruct((tokens, side), bf)),
+        in_specs=[pl.BlockSpec(memory_space=pltpu.SMEM)] + [vmem] * 9,
+        out_specs=[vmem, vmem],
+        scratch_shapes=[
+            pltpu.VMEM((tokens, width), bf),
+            pltpu.VMEM((4 * tokens, side), bf),
+            pltpu.VMEM((4 * tokens, side), bf),
+            pltpu.VMEM((tokens, side), bf),
+            pltpu.VMEM((2 * tokens, side), bf),
+            pltpu.VMEM((2 * tokens, side), bf),
+            pltpu.VMEM((tokens, side), bf),
+            pltpu.VMEM((tokens, side), bf),
+        ],
+        compiler_params=pltpu.CompilerParams(vmem_limit_bytes=56 * 1024 * 1024),
+    )(slots, x, part, far, farpart, xz, gain, w_qkv, own, ant)
+
+
+def placement(block_cols, antipode, cycles, lons):
+    cap_half = lax.axis_index("lat") % 2
+    blocks = cycles // BM
+    picks = lax.dynamic_slice_in_dim(block_cols, cap_half * blocks, blocks, 0)
+    cap_block = jnp.where(picks >= 2 * blocks, picks - 2 * blocks, 2 * blocks - 1 - picks)
+    slots = (
+        jnp.where(picks >= 2 * blocks, 0, 2 * blocks)
+        + jnp.where(cap_block // blocks == cap_half, 0, blocks)
+        + cap_block % blocks
+    )
+    shape = (blocks, lons // 8, BM, 8)
+    axis = [lax.broadcasted_iota(jnp.int32, shape, n) for n in range(4)]
+    cycle = axis[0] * BM + axis[2]
+    own = cycle * lons + axis[1] * 8 + axis[3]
+    far = cycle * lons + (antipode % lons).reshape(1, lons // 8, 1, 8)
+    return slots.astype(jnp.int32), own.reshape(-1, 1), far.reshape(-1, 1)
+
+
+def on_device_halves(field, norm_gain, w_qkv, w_out, block_cols, antipode):
+    cycles, lons, width = field.shape
+    tokens = cycles * lons
+    slots, own, ant = placement(block_cols, antipode, cycles, lons)
+    xz, part, far, farpart = exchange(field)
+    flat = [a.reshape(-1, width) for a in (field, part, far, farpart, xz)]
+    zonal, column = attend(slots, *flat, norm_gain.reshape(1, width), w_qkv, own, ant)
+    back = giveback(zonal.reshape(GROUP, cycles // GROUP, lons, HZ * HD)).reshape(tokens, HZ * HD)
+    total = jnp.dot(back, w_out[: HZ * HD], preferred_element_type=jnp.float32)
+    total = total + jnp.dot(column, w_out[HZ * HD :], preferred_element_type=jnp.float32)
+    return total.astype(jnp.bfloat16).reshape(cycles, lons, width)
+
+
 def solution(mesh):
     in_specs = (P("lat", "lon", None), P(), P(), P(), P(), P("lon"))
     out_specs = P("lat", "lon", None)
+    halves = mesh.shape["lat"] == 4 and mesh.shape["lon"] == 2 * GROUP
     return jax.shard_map(
-        on_device, mesh=mesh, in_specs=in_specs, out_specs=out_specs, check_vma=False
-    )
+        on_device_halves if halves else on_device,
+        mesh=mesh,
+        in_specs=in_specs,
+        out_specs=out_specs,
+        check_vma=False,
+    )

time: 215 us -> 113 us (0.53)
  Pallas kernels: 0 us -> 105 us
  local copies, waits for them, and re-layouts: 72.5 us -> 1.77 us
  waiting for transfers between devices: 45.1 us -> 0 us
  blocking collectives: 39.2 us -> 0 us
  other arithmetic: 24.5 us -> 2.03 us
  matrix products: 22.2 us -> 3.53 us
  starting transfers between devices: 10.4 us -> 0 us
    pallas_call x0 -> x3, Pallas kernels: none -> 105 us  [the longest x1 61.7 us: exchange(): pl.pallas_call(exchange_kernel, name='exchange', out_shape=(jax.ShapeDtyp...]
    all_to_all x2 -> x0, blocking collectives: 39.2 us -> none  [the longest x1 21.6 us: on_device(): lax.all_to_all(zonal_part[1], 'lon', split_axis=0, concat_axis=1, tiled=T...]
    all_to_all x2 -> x0, waiting for transfers between devices: 30.4 us -> none  [the longest x1 30.4 us: on_device(): lax.all_to_all(zonal_part[0], 'lon', split_axis=0, concat_axis=1, tiled=T...]
    reshape x7 -> x0, local copies, waits for them, and re-layouts: 19 us -> none  [the longest x1 11.2 us: on_device(): column = column.reshape(block_total, BM, lon_count, 2, column_heads, HD)]
    select_n x3 -> x0, local copies, waits for them, and re-layouts: 18.5 us -> none  [the longest x2 16 us: on_device(): jnp.take(column, picked, axis=0)]
    select_n x4 -> x1, other arithmetic: 15.8 us -> 0.66 us  [placement(): far = cycle * lons + (antipode % lons).reshape(1, lons // 8, 1, 8)]
    gather x3 -> x0, local copies, waits for them, and re-layouts: 15.1 us -> none  [the longest x2 12.8 us: on_device(): jnp.take(column, picked, axis=0)]
    ppermute x3 -> x0, waiting for transfers between devices: 14.7 us -> none  [the longest x1 14.7 us: shifted(): lax.ppermute(shard, axis, [(i, (i + by) % devices) for i in range(devices)])]
  transfers between devices with their start and end apart: 5 -> 0, of which waited for: 2 -> 0; matrix products, arithmetic and copies ran while one was open for 10% -> 0% of each run, Pallas kernels for 0% -> 0%
where the time goes in v1:
time: 113 us
  Pallas kernels  105 us (93%)
  matrix products  3.53 us (3%)
  other arithmetic  2.03 us (2%)
  local copies, waits for them, and re-layouts  1.77 us (2%)
    pallas_call x1, Pallas kernels, exchange(): pl.pallas_call(exchange_kernel, name='exchange', out_shape=(jax.ShapeDtyp...  61.7 us
    pallas_call x1, Pallas kernels, attend(): pl.pallas_call(attend_kernel, name='attend', out_shape=(jax.ShapeDtypeStr...  35.3 us
    pallas_call x1, Pallas kernels, giveback(): pl.pallas_call(giveback_kernel, name='giveback', out_shape=jax.ShapeDtype...  8.52 us

profile of v1, /device:TPU:0, one launch (start us, length us, event | category | flops | bytes accessed | tf_op | source)
XLA Modules:
  0.0 112.9 jit_solution(3419028480832611275)
XLA Ops:
  0.0 1.3 %fusion.5.slots_ref = s32[2,4]{1,0:T(2,128)} fusion(s32[4,4]{1,0:T(4,128)} %param.10, s32[]{:T(128)S(6)} %select_n.38, s32[]{:T(128)S(6)} %select_n.37), kind=kLoop, calls=%fused_computation.17 | loop fusion | flops 224 | bytes 72 | tf_op jit(solution)/shard_map/add | solution.py:431
  1.3 0.7 and_select_fusion
  2.0 0.1 add.101
  2.0 0.1 fusion.3
  2.1 0.8 add.107.ant_ref
  3.0 0.8 add.106.own_ref
  3.8 61.7 %exchange.1 = (bf16[2,4,4,32,1024]{4,3,2,1,0:T(8,128)(2,1)}, bf16[16,32,1024]{2,1,0:T(8,128)(2,1)}, bf16[16,32,1024]{2,1,0:T(8,128)(2,1)}, bf16[16,32,1024]{2,1,0:T(8,128)(2,1)}) custom-call(bf16[16,32,1024]{2,1,0:T(8,128)(2,1)} %x_ref.1), custom_call_target="tpu_custom_call" | custom-call | tf_op jit(solution)/shard_map/exchange/pallas_call | solution.py:211
  65.5 0.0 copy-start
  65.5 35.3 %attend.1 = (bf16[512,512]{1,0:T(8,128)(2,1)}, bf16[512,512]{1,0:T(8,128)(2,1)}) custom-call(s32[2,4]{1,0:T(2,128)} %fusion.5.slots_ref, bf16[512,1024]{1,0:T(8,128)(2,1)} %bitcast.15, bf16[512,1024]{1,0:T(8,128)(2,1)} %bitcast.18, bf16[512,1024]{1,0:T(8,128)(2,1)} %bitcast.19, bf16[512,1024]{1,0:T(8,128)(2,1)} %bitcast.20, bf16[1024,1024]{1,0:T(8,128)(2,1)} %bitcast.16, ...), custom_call_target="tpu_custom_call" | custom-call | tf_op jit(solution)/shard_map/attend/pallas_call | solution.py:405
  100.8 8.5 %giveback.1 = bf16[16,32,512]{2,1,0:T(8,128)(2,1)} custom-call(bf16[4,4,32,512]{3,2,1,0:T(8,128)(2,1)} %bitcast.21), custom_call_target="tpu_custom_call" | custom-call | tf_op jit(solution)/shard_map/giveback/pallas_call | solution.py:260
  109.3 0.0 copy-start.1
  109.3 0.0 copy-done
  109.3 1.8 %fusion.1 = f32[512,1024]{1,0:T(8,128)S(1)} fusion(bf16[512,512]{1,0:T(8,128)(2,1)} %bitcast.17, bf16[1024,1024]{1,0:T(8,128)(2,1)S(1)} %copy-done), kind=kOutput, calls=%fused_computation.2 | convolution fusion | flops 536870912 | bytes 3670016 | tf_op jit(solution)/shard_map/dot_general | solution.py:451
  111.1 0.0 copy-done.1
  111.1 1.7 %add_convert_fusion = bf16[512,1024]{1,0:T(8,128)(2,1)} fusion(f32[512,1024]{1,0:T(8,128)S(1)} %fusion.1, bf16[512,512]{1,0:T(8,128)(2,1)S(1)} %copy-done.1, bf16[1024,1024]{1,0:T(8,128)(2,1)S(1)} %copy-done), kind=kOutput, calls=%fused_computation | convolution fusion | flops 537919488 | bytes 4718592 | tf_op jit(solution)/shard_map/dot_general | solution.py:452
  (2 shorter events, 0.0 us)
Async XLA Ops:
  65.5 43.8 %copy-start = (bf16[1024,1024]{1,0:T(8,128)(2,1)S(1)}, bf16[1024,1024]{1,0:T(8,128)(2,1)}, u32[]{:S(2)}) copy-start(bf16[1024,1024]{1,0:T(8,128)(2,1)} %param.9) | copy-start | bytes 6291460
  109.3 1.8 %copy-start.1 = (bf16[512,512]{1,0:T(8,128)(2,1)S(1)}, bf16[512,512]{1,0:T(8,128)(2,1)}, u32[]{:S(2)}) copy-start(bf16[512,512]{1,0:T(8,128)(2,1)} %get-tuple-element.16) | copy-start | bytes 1572868

commit v2 on v0

--- a/solution.py
+++ b/solution.py
@@ -1,6 +1,10 @@
+import functools
+
 import jax
 import jax.numpy as jnp
 from jax import lax
+from jax.experimental import pallas as pl
+from jax.experimental.pallas import tpu as pltpu
 from jax.sharding import PartitionSpec as P
 
 HEADS = 16
@@ -134,9 +138,347 @@
     return total.astype(jnp.bfloat16)
 
 
+GROUP = 4
+MESH = pl.DeviceIdType.MESH
+
+
+def norm_rows(x, gain):
+    values = x.astype(jnp.float32)
+    mean = jnp.mean(values * values, axis=-1, keepdims=True)
+    return (values * lax.rsqrt(mean + epsilon) * gain).astype(jnp.bfloat16)
+
+
+def mm(a, b):
+    return jnp.dot(a, b, preferred_element_type=jnp.float32).astype(jnp.bfloat16)
+
+
+def pair_attend(q, k, v, mask):
+    rows = q.shape[0]
+    first = lax.broadcasted_iota(jnp.int32, q.shape, 1) < HD
+    q = q * jnp.asarray(HD ** (-0.5), q.dtype)
+    zero = jnp.zeros_like(q)
+    stacked = jnp.concatenate([jnp.where(first, q, zero), jnp.where(first, zero, q)], axis=0)
+    scores = lax.dot_general(stacked, k, (((1,), (1,)), ((), ())), preferred_element_type=jnp.float32)
+    if mask is not None:
+        scores = jnp.where(mask, scores, -jnp.inf)
+    exponent = jnp.exp(scores - jnp.max(scores, axis=-1, keepdims=True))
+    weights = (exponent * (1.0 / jnp.sum(exponent, axis=-1, keepdims=True))).astype(jnp.bfloat16)
+    out = jnp.dot(weights, v, preferred_element_type=jnp.float32)
+    return jnp.where(first, out[:rows], out[rows:]).astype(jnp.bfloat16)
+
+
+def one_hot(hit):
+    return jnp.where(hit, 1.0, 0.0).astype(jnp.bfloat16)
+
+
+def iota(shape, axis):
+    return lax.broadcasted_iota(jnp.int32, shape, axis)
+
+
+def rows_at(start, size, step=None):
+    return pl.ds(pl.multiple_of(start, step or size), size)
+
+
+def layer_kernel(
+    block_cols, ant_ref, gain_ref, x_hbm, w_hbm, wo_hbm, out_ref,
+    xo, part, far, farpart, xz, w, wo, xn, kc, vc, qc, kz, vz, qz, zo, zret, oc, place, place_far,
+    send, recv, local,
+):
+    lat, lon = lax.axis_index("lat"), lax.axis_index("lon")
+    half, q = lon // GROUP, lon % GROUP
+    cap_half = lat % 2
+    anti = (1 - half) * GROUP + q
+    mate = lat + 1 - 2 * cap_half
+    steps, lons, width = x_hbm.shape[1:]
+    side = HZ * HD
+    span = GROUP * lons
+    block = BM * lons
+    blocks = GROUP * steps // BM
+    groups = lons // 8
+    gain = gain_ref[...]
+
+    def peer(k):
+        return lax.rem(q + k, GROUP)
+
+    def remote(src, dst, n, lat_id, lon_id):
+        return pltpu.make_async_remote_copy(
+            src_ref=src,
+            dst_ref=dst,
+            send_sem=send.at[n],
+            recv_sem=recv.at[n],
+            device_id=(lat_id, lon_id),
+            device_id_type=MESH,
+        )
+
+    def to_peer(src, dst, n, k):
+        return remote(src, dst, n, lat, half * GROUP + peer(k))
+
+    def far_copy(j):
+        return remote(x_hbm.at[:, j], far.at[:, j], j, lat, anti)
+
+    def near_copy(k):
+        return to_peer(x_hbm.at[peer(k)], xz.at[:, 0, q], 3 + k, k)
+
+    def pass_copy(j, k):
+        return to_peer(far.at[peer(k), j], xz.at[j, 1, q], 8 + 3 * j + k - 1, k)
+
+    def mate_copy(j):
+        return remote(far.at[:, j], farpart.at[:, j], 20 + j, mate, lon)
+
+    def back_copy(j, k):
+        return to_peer(zo.at[j, peer(k)], zret.at[q, j], 24 + 3 * j + k - 1, k)
+
+    def own_pass(j):
+        return pltpu.make_async_copy(far.at[q, j], xz.at[j, 1, q], local.at[4 + j])
+
+    def own_back(j):
+        return pltpu.make_async_copy(zo.at[j, q], zret.at[q, j], local.at[8 + j])
+
+    others = (1, 2, 3)
+    barrier = pltpu.get_barrier_semaphore()
+    partners = [(lat, anti), (mate, lon)] + [(lat, half * GROUP + peer(k)) for k in others]
+    for a, b in partners:
+        pl.semaphore_signal(barrier, inc=1, device_id=(a, b), device_id_type=MESH)
+    load_x = pltpu.make_async_copy(x_hbm, xo, local.at[0])
+    load_w = pltpu.make_async_copy(w_hbm, w, local.at[1])
+    load_wo = pltpu.make_async_copy(wo_hbm, wo, local.at[2])
+    own_near = pltpu.make_async_copy(x_hbm.at[q], xz.at[:, 0, q], local.at[3])
+    load_x.start()
+    load_w.start()
+    pl.semaphore_wait(barrier, len(partners))
+    for j in range(steps):
+        far_copy(j).start()
+    pair = remote(x_hbm, part, 7, mate, lon)
+    pair.start()
+    for k in others:
+        near_copy(k).start()
+    own_near.start()
+    load_wo.start()
+
+    def weight(which, zone):
+        first = which * width + zone * side
+        return w[:, first : first + side]
+
+    token, slot = iota((block, block), 1), iota((block, block), 0)
+    want = (slot // 8 % BM) * lons + (slot // (8 * BM)) * 8 + slot % 8
+    place[...] = one_hot(token == want)
+    perm = lax.rem(ant_ref[...], lons)
+    lon_hot = one_hot(iota((lons, lons), 0) == perm)
+    t = iota((span, lons), 0)
+    spread = one_hot((t // 16 % groups) * 8 + t % 8 == iota((span, lons), 1))
+    moved = lax.dot_general(spread, lon_hot, (((1,), (1,)), ((), ())), preferred_element_type=jnp.float32)
+    tile = one_hot(iota((lons, span), 0) == iota((lons, span), 1) % lons)
+    wide = jnp.dot(moved.astype(jnp.bfloat16), tile, preferred_element_type=jnp.float32)
+    t, src = iota((span, span), 0), iota((span, span), 1)
+    same = 2 * (t // (16 * groups)) + t // 8 % 2 == src // lons
+    place_far[...] = jnp.where(same, wide, 0.0).astype(jnp.bfloat16)
+
+    def column_source(ref, s):
+        @pl.loop(0, blocks)
+        def _(i):
+            for c in range(0, BM, 2):
+                piece = ref[i * (BM // steps) + c // steps, pl.ds(c % steps, 2)]
+                xn[c * lons : (c + 2) * lons, :] = norm_rows(piece.reshape(2 * lons, width), gain)
+            placed = mm(place[...], xn[0:block, :])
+            to = rows_at((s * blocks + i) * block, block)
+            kc[to, :] = mm(placed, weight(1, 1))
+            vc[to, :] = mm(placed, weight(2, 1))
+            if s == 0:
+                qc[rows_at(i * block, block), :] = mm(placed, weight(0, 1))
+
+    load_x.wait()
+    load_w.wait()
+    column_source(xo, 0)
+    pair.wait_recv()
+    column_source(part, 1)
+    for k in others:
+        near_copy(k).wait_recv()
+    own_near.wait()
+
+    def cycle_norm(j, h):
+        for m in range(0, GROUP, 2):
+            piece = xz[j, h, pl.ds(m, 2)].reshape(2 * lons, width)
+            xn[m * lons : (m + 2) * lons, :] = norm_rows(piece, gain)
+
+    def arrive(j):
+        far_copy(j).wait_recv()
+        for k in others:
+            pass_copy(j, k).start()
+        own_pass(j).start()
+        mate_copy(j).start()
+
+    arrive(0)
+
+    @pl.loop(0, steps)
+    def _(j):
+        cycle_norm(j, 0)
+        placed = xn[0:span, :]
+        kz[j, 0:span, :] = mm(placed, weight(1, 0))
+        vz[j, 0:span, :] = mm(placed, weight(2, 0))
+        qz[j] = mm(placed, weight(0, 0))
+
+    @pl.loop(0, steps)
+    def _(j):
+        @pl.when(j > 0)
+        def _():
+            arrive(j)
+            for k in others:
+                back_copy(j - 1, k).start()
+            own_back(j - 1).start()
+
+        mate_copy(j).wait_recv()
+        for s, ref in ((0, far), (1, farpart)):
+            for p in range(0, GROUP, 2):
+                piece = ref[pl.ds(p, 2), j].reshape(2 * lons, width)
+                xn[s * span + p * lons : s * span + (p + 2) * lons, :] = norm_rows(piece, gain)
+        placed = jnp.concatenate(
+            [mm(place_far[...], xn[0:span, :]), mm(place_far[...], xn[span : 2 * span, :])], axis=0
+        )
+        for which, ref in ((1, kc), (2, vc)):
+            made = mm(placed, weight(which, 1))
+            for n in range(2 * blocks * groups):
+                to = rows_at((2 * blocks * groups + n) * 8 * BM + j * 16, 16)
+                ref[to, :] = made[n * 16 : (n + 1) * 16]
+        for k in others:
+            pass_copy(j, k).wait_recv()
+        own_pass(j).wait()
+        cycle_norm(j, 1)
+        placed = xn[0:span, :]
+        kz[j, span : 2 * span, :] = mm(placed, weight(1, 0))
+        vz[j, span : 2 * span, :] = mm(placed, weight(2, 0))
+        for p in range(side // 128):
+            cols = slice(p * 128, (p + 1) * 128)
+            out = pair_attend(qz[j, :, cols], kz[j, :, cols], vz[j, :, cols], None)
+            zo[j, :, :, cols] = out.reshape(GROUP, lons, 128)
+
+    rows = 8 * BM
+    mask = iota((2 * rows, 4 * rows), 0) % 8 == iota((2 * rows, 4 * rows), 1) % 8
+
+    @pl.loop(0, blocks * groups)
+    def _(n):
+        @pl.when(n == 1)
+        def _():
+            for k in others:
+                back_copy(steps - 1, k).start()
+            own_back(steps - 1).start()
+
+        b, g = n // groups, lax.rem(n, groups)
+        first = 2 * blocks
+        held = [cap_half * blocks + i for i in range(blocks)]
+        held += [(1 - cap_half) * blocks + i for i in range(blocks)]
+        held = [first + c for c in held] + [first - 1 - c for c in held]
+        picks = [block_cols[cap_half * blocks + b, m] for m in range(4)]
+        chosen = [[pick == name for name in held] for pick in picks]
+        at = rows_at(n * rows, rows)
+
+        def selected(ref, cols):
+            pieces = [ref[rows_at((s * groups + g) * rows, rows), cols] for s in range(2 * first)]
+            parts = []
+            for flags in chosen:
+                result = pieces[0]
+                for flag, piece in zip(flags[1:], pieces[1:]):
+                    result = lax.select_n(flag, result, piece)
+                parts.append(result)
+            return jnp.concatenate(parts, axis=0)
+
+        for p in range(side // 128):
+            cols = slice(p * 128, (p + 1) * 128)
+            oc[at, cols] = pair_attend(qc[at, cols], selected(kc, cols), selected(vc, cols), mask)
+
+    for j in range(steps):
+        for k in others:
+            back_copy(j, k).wait_recv()
+        own_back(j).wait()
+    load_wo.wait()
+
+    @pl.loop(0, blocks)
+    def _(i):
+        at = rows_at(i * block, block)
+        column = lax.dot_general(
+            place[...], oc[at, :], (((0,), (0,)), ((), ())), preferred_element_type=jnp.float32
+        ).astype(jnp.bfloat16)
+        many = BM // steps
+        zonal = zret[pl.ds(i * many, many)].reshape(block, side)
+        total = jnp.dot(zonal, wo[0:side, :], preferred_element_type=jnp.float32)
+        total += jnp.dot(column, wo[side : 2 * side, :], preferred_element_type=jnp.float32)
+        out_ref[at, :] = total.astype(jnp.bfloat16)
+
+    for j in range(steps):
+        far_copy(j).wait_send()
+        mate_copy(j).wait_send()
+        for k in others:
+            pass_copy(j, k).wait_send()
+            back_copy(j, k).wait_send()
+    pair.wait_send()
+    for k in others:
+        near_copy(k).wait_send()
+
+
+def on_device_halves(field, norm_gain, w_qkv, w_out, block_cols, antipode):
+    cycles, lons, width = field.shape
+    tokens = cycles * lons
+    steps = cycles // GROUP
+    side = HZ * HD
+    span = GROUP * lons
+    block = BM * lons
+    bf = jnp.bfloat16
+    anywhere = pl.BlockSpec(memory_space=pl.ANY)
+    vmem = pl.BlockSpec(memory_space=pltpu.VMEM)
+    shapes = [
+        (GROUP, steps, lons, width),
+        (GROUP, steps, lons, width),
+        (GROUP, steps, lons, width),
+        (GROUP, steps, lons, width),
+        (steps, 2, GROUP, lons, width),
+        (width, 3 * width),
+        (width, width),
+        (2 * block, width),
+        (4 * tokens, side),
+        (4 * tokens, side),
+        (tokens, side),
+        (steps, 2 * span, side),
+        (steps, 2 * span, side),
+        (steps, span, side),
+        (steps, GROUP, lons, side),
+        (GROUP, steps, lons, side),
+        (tokens, side),
+        (block, block),
+        (span, span),
+    ]
+    out = pl.pallas_call(
+        layer_kernel,
+        name="layer",
+        out_shape=jax.ShapeDtypeStruct((tokens, width), bf),
+        in_specs=[pl.BlockSpec(memory_space=pltpu.SMEM), vmem, vmem, anywhere, anywhere, anywhere],
+        out_specs=vmem,
+        scratch_shapes=[pltpu.VMEM(shape, bf) for shape in shapes]
+        + [
+            pltpu.SemaphoreType.DMA((36,)),
+            pltpu.SemaphoreType.DMA((36,)),
+            pltpu.SemaphoreType.DMA((12,)),
+        ],
+        compiler_params=pltpu.CompilerParams(
+            collective_id=0, has_side_effects=True, vmem_limit_bytes=56 * 1024 * 1024
+        ),
+    )(
+        block_cols,
+        antipode.reshape(1, lons),
+        norm_gain.reshape(1, width),
+        field.reshape(GROUP, steps, lons, width),
+        w_qkv,
+        w_out,
+    )
+    return out.reshape(cycles, lons, width)
+
+
 def solution(mesh):
     in_specs = (P("lat", "lon", None), P(), P(), P(), P(), P("lon"))
     out_specs = P("lat", "lon", None)
+    halves = mesh.shape["lat"] == 4 and mesh.shape["lon"] == 2 * GROUP
     return jax.shard_map(
-        on_device, mesh=mesh, in_specs=in_specs, out_specs=out_specs, check_vma=False
-    )
+        on_device_halves if halves else on_device,
+        mesh=mesh,
+        in_specs=in_specs,
+        out_specs=out_specs,
+        check_vma=False,
+    )

time: 215 us -> 88.8 us (0.41)
  Pallas kernels: 0 us -> 86.3 us
  local copies, waits for them, and re-layouts: 72.5 us -> 2.29 us
  waiting for transfers between devices: 45.1 us -> 0 us
  blocking collectives: 39.2 us -> 0 us
  other arithmetic: 24.5 us -> 0 us
  matrix products: 22.2 us -> 0 us
  starting transfers between devices: 10.4 us -> 0 us
    pallas_call x0 -> x1, Pallas kernels: none -> 86.3 us  [on_device_halves(): pl.pallas_call(layer_kernel, name='layer', out_shape=jax.ShapeDtypeStruct...]
    all_to_all x2 -> x0, blocking collectives: 39.2 us -> none  [the longest x1 21.6 us: on_device(): lax.all_to_all(zonal_part[1], 'lon', split_axis=0, concat_axis=1, tiled=T...]
    all_to_all x2 -> x0, waiting for transfers between devices: 30.4 us -> none  [the longest x1 30.4 us: on_device(): lax.all_to_all(zonal_part[0], 'lon', split_axis=0, concat_axis=1, tiled=T...]
    reshape x7 -> x0, local copies, waits for them, and re-layouts: 19 us -> none  [the longest x1 11.2 us: on_device(): column = column.reshape(block_total, BM, lon_count, 2, column_heads, HD)]
    select_n x3 -> x0, local copies, waits for them, and re-layouts: 18.5 us -> none  [the longest x2 16 us: on_device(): jnp.take(column, picked, axis=0)]
    select_n x4 -> x0, other arithmetic: 15.8 us -> none  [the longest x1 6.22 us: on_device(): jnp.take(column, picked, axis=0)]
    dot_general x8 -> x0, matrix products: 15.4 us -> none  [the longest x2 5.05 us: on_device(): jnp.einsum('lhqk,klhd->qlhd', soft_weights, chosen[:, :, 1], preferred_el...]
    gather x3 -> x0, local copies, waits for them, and re-layouts: 15.1 us -> none  [the longest x2 12.8 us: on_device(): jnp.take(column, picked, axis=0)]
  transfers between devices with their start and end apart: 5 -> 0, of which waited for: 2 -> 0; matrix products, arithmetic and copies ran while one was open for 10% -> 0% of each run, Pallas kernels for 0% -> 0%
where the time goes in v2:
time: 88.8 us; the launch traced here: 88.6 us
  Pallas kernels  86.3 us (97%)
  local copies, waits for them, and re-layouts  2.29 us (3%)
    pallas_call x1, Pallas kernels, on_device_halves(): pl.pallas_call(layer_kernel, name='layer', out_shape=jax.ShapeDtypeStruct...  86.3 us
    unnamed x1, local copies, waits for them, and re-layouts  2.29 us

profile of v2, /device:TPU:0, one launch (start us, length us, event | category | flops | bytes accessed | tf_op | source)
XLA Modules:
  0.0 88.6 jit_solution(13299559194082170330)
XLA Ops:
  0.0 86.3 %layer.1 = bf16[512,1024]{1,0:T(8,128)(2,1)} custom-call(s32[4,4]{1,0:T(4,128)} %block_cols.1, s32[1,32]{1,0:T(1,128)} %bitcast.7, f32[1,1024]{1,0:T(1,128)} %bitcast.6, bf16[4,4,32,1024]{3,2,1,0:T(8,128)(2,1)} %bitcast.5, bf16[1024,3072]{1,0:T(8,128)(2,1)} %w_hbm.1, bf16[1024,1024]{1,0:T(8,128)(2,1)} %wo_hbm.1), custom_call_target="tpu_custom_call" | custom-call | tf_op jit(solution)/shard_map/layer/pallas_call | solution.py:448
  86.4 2.3 %copy.8 = bf16[16,32,1024]{2,1,0:T(8,128)(2,1)} copy(bf16[16,32,1024]{2,1,0:T(8,128)(2,1)} %bitcast.4) | data formatting | bytes 2097152

commit v3 on v2

--- a/solution.py
+++ b/solution.py
@@ -180,8 +180,8 @@
 
 
 def layer_kernel(
-    block_cols, ant_ref, gain_ref, x_hbm, w_hbm, wo_hbm, out_ref,
-    xo, part, far, farpart, xz, w, wo, xn, kc, vc, qc, kz, vz, qz, zo, zret, oc, place, place_far,
+    block_cols, ant_ref, gain_ref, x_hbm, w_hbm, out_ref,
+    xo, part, far, farpart, xz, w, xn, kc, vc, qc, kz, vz, qz, zo, zret, oc, place, place_far,
     send, recv, local,
 ):
     lat, lon = lax.axis_index("lat"), lax.axis_index("lon")
@@ -241,19 +241,17 @@
         pl.semaphore_signal(barrier, inc=1, device_id=(a, b), device_id_type=MESH)
     load_x = pltpu.make_async_copy(x_hbm, xo, local.at[0])
     load_w = pltpu.make_async_copy(w_hbm, w, local.at[1])
-    load_wo = pltpu.make_async_copy(wo_hbm, wo, local.at[2])
     own_near = pltpu.make_async_copy(x_hbm.at[q], xz.at[:, 0, q], local.at[3])
     load_x.start()
     load_w.start()
     pl.semaphore_wait(barrier, len(partners))
-    for j in range(steps):
-        far_copy(j).start()
     pair = remote(x_hbm, part, 7, mate, lon)
-    pair.start()
+    far_copy(0).start()
+    far_copy(1).start()
     for k in others:
         near_copy(k).start()
+    pair.start()
     own_near.start()
-    load_wo.start()
 
     def weight(which, zone):
         first = which * width + zone * side
@@ -306,6 +304,11 @@
             pass_copy(j, k).start()
         own_pass(j).start()
         mate_copy(j).start()
+
+        @pl.when(j + 2 < steps)
+        def _():
+            far_copy(j + 2).start()
+
 
     arrive(0)
 
@@ -389,7 +392,6 @@
         for k in others:
             back_copy(j, k).wait_recv()
         own_back(j).wait()
-    load_wo.wait()
 
     @pl.loop(0, blocks)
     def _(i):
@@ -399,9 +401,8 @@
         ).astype(jnp.bfloat16)
         many = BM // steps
         zonal = zret[pl.ds(i * many, many)].reshape(block, side)
-        total = jnp.dot(zonal, wo[0:side, :], preferred_element_type=jnp.float32)
-        total += jnp.dot(column, wo[side : 2 * side, :], preferred_element_type=jnp.float32)
-        out_ref[at, :] = total.astype(jnp.bfloat16)
+        out_ref[at, 0:side] = zonal
+        out_ref[at, side : 2 * side] = column
 
     for j in range(steps):
         far_copy(j).wait_send()
@@ -431,7 +432,6 @@
         (GROUP, steps, lons, width),
         (steps, 2, GROUP, lons, width),
         (width, 3 * width),
-        (width, width),
         (2 * block, width),
         (4 * tokens, side),
         (4 * tokens, side),
@@ -448,8 +448,8 @@
     out = pl.pallas_call(
         layer_kernel,
         name="layer",
-        out_shape=jax.ShapeDtypeStruct((tokens, width), bf),
-        in_specs=[pl.BlockSpec(memory_space=pltpu.SMEM), vmem, vmem, anywhere, anywhere, anywhere],
+        out_shape=jax.ShapeDtypeStruct((tokens, 2 * side), bf),
+        in_specs=[pl.BlockSpec(memory_space=pltpu.SMEM), vmem, vmem, anywhere, anywhere],
         out_specs=vmem,
         scratch_shapes=[pltpu.VMEM(shape, bf) for shape in shapes]
         + [
@@ -466,8 +466,8 @@
         norm_gain.reshape(1, width),
         field.reshape(GROUP, steps, lons, width),
         w_qkv,
-        w_out,
-    )
+    )
+    out = jnp.dot(out, w_out, preferred_element_type=jnp.float32).astype(bf)
     return out.reshape(cycles, lons, width)
 
 

time: 88.8 us -> 74.3 us (0.84)
  Pallas kernels: 86.3 us -> 70.7 us
  matrix products: 0 us -> 3.45 us
  local copies, waits for them, and re-layouts: 2.29 us -> 0.01 us
    pallas_call x1, Pallas kernels: 86.3 us -> 70.7 us  [on_device_halves(): pl.pallas_call(layer_kernel, name='layer', out_shape=jax.ShapeDtypeStruct...]
    dot_general x0 -> x1, matrix products: none -> 3.45 us  [on_device_halves(): out = jnp.dot(out, w_out, preferred_element_type=jnp.float32).astype(bf)]
    unnamed x1 -> x2, local copies, waits for them, and re-layouts: 2.29 us -> 0.01 us
where the time goes in v3:
time: 74.3 us; the launch traced here: 74.1 us
  Pallas kernels  70.7 us (95%)
  matrix products  3.45 us (5%)
    pallas_call x1, Pallas kernels, on_device_halves(): pl.pallas_call(layer_kernel, name='layer', out_shape=jax.ShapeDtypeStruct...  70.7 us
    dot_general x1, matrix products, on_device_halves(): out = jnp.dot(out, w_out, preferred_element_type=jnp.float32).astype(bf)  3.45 us

profile of v3, /device:TPU:0, one launch (start us, length us, event | category | flops | bytes accessed | tf_op | source)
XLA Modules:
  0.0 74.1 jit_solution(3980377074360704311)
XLA Ops:
  0.0 0.0 copy-start
  0.0 70.7 %layer.1 = bf16[512,1024]{1,0:T(8,128)(2,1)} custom-call(s32[4,4]{1,0:T(4,128)} %block_cols.1, s32[1,32]{1,0:T(1,128)} %bitcast.8, f32[1,1024]{1,0:T(1,128)} %bitcast.7, bf16[4,4,32,1024]{3,2,1,0:T(8,128)(2,1)} %bitcast.6, bf16[1024,3072]{1,0:T(8,128)(2,1)} %w_hbm.1), custom_call_target="tpu_custom_call" | custom-call | tf_op jit(solution)/shard_map/layer/pallas_call | solution.py:448
  70.7 0.0 copy-done
  70.7 3.4 %convolution_convert_fusion = bf16[512,1024]{1,0:T(8,128)(2,1)} fusion(bf16[512,1024]{1,0:T(8,128)(2,1)} %layer.1, bf16[1024,1024]{1,0:T(8,128)(2,1)S(1)} %copy-done), kind=kOutput, calls=%fused_computation | convolution fusion | flops 1074266112 | bytes 4194304 | tf_op jit(solution)/shard_map/dot_general | solution.py:470
Async XLA Ops:
  0.0 70.7 %copy-start = (bf16[1024,1024]{1,0:T(8,128)(2,1)S(1)}, bf16[1024,1024]{1,0:T(8,128)(2,1)}, u32[]{:S(2)}) copy-start(bf16[1024,1024]{1,0:T(8,128)(2,1)} %param.9) | copy-start | bytes 6291460
